TPU v7x, 32 devices: a whole 2x2x4 slice. The times are simulated.
32 devices in a mesh: grp: 2 (over x), sub: 16 (over z, y, core).
Axes of the slice: x: 2, y: 2, z: 4, core: 2. Of those that a mesh axis runs over, the one named last changes fastest.
Arguments:
- load_cases: float32 [36864, 128], P(('grp', 'sub')), may hold values from -6 to 6
- schur_matrix: float32 [36864, 1152], P(('grp', 'sub')), may hold values from -0.0017361111 to 16, as said below
- local_inverse: float32 [36864, 1152], P(('grp', 'sub')), may hold values from -0.00021701389 to 2, as said below
- coarse_basis: float32 [1024, 1152], P(('grp', 'sub')), may hold values from -0.375 to 0.375
- group_inverse: float32 [1024, 512], P(('grp', 'sub')), may hold values from -0.0009765625 to 4, as said below
- group_modes: float32 [1024, 32], P(('grp', 'sub')), may hold values from -0.375 to 0.375
- top_inverse: float32 [64, 64], replicated, may hold values from -0.0078125 to 4, as said below
- face_map: int32 [32, 1152], P(('grp', 'sub')), may hold values from 0 to 1151, each once within a row
- spectrum: float32 [2], replicated, may hold values from 0.1 to 6, as said below
Outputs:
- solution: float32 [36864, 128], P(('grp', 'sub'))
- residual: float32 [36864, 128], P(('grp', 'sub'))
Inputs may be any that keep to these rules, and one draw needn't show every extreme that they name: `face_map`: each row is a permutation of 0 to 1151. `schur_matrix`: each subdomain's 1152 x 1152 block is symmetric positive definite. `local_inverse`: each subdomain's 1152 x 1152 block is symmetric positive definite. `group_inverse`: each group's 512 x 512 block is symmetric positive definite. `top_inverse`: symmetric positive definite. spectrum[0] < spectrum[1].
All inputs are finite; a program needn't handle non-finite values.
Results may differ from a plain program's by a relative error of at most 0.00011.
Values sent between devices are 32-bit elements; how exact they have to be, the bound alone decides.
A program may use at most 64 MiB of HBM per device.

v0:
```python
import functools

import jax
import jax.numpy as jnp
from jax import lax
from jax.experimental import pallas as pl
from jax.experimental.pallas import tpu as pltpu
from jax.sharding import PartitionSpec as P

ITERS = 3
F32 = jnp.float32
BF16 = jnp.bfloat16
MESH = pl.DeviceIdType.MESH


def dot(a, b):
    return jnp.dot(a, b, preferred_element_type=F32)


def exact_dot(a, b):
    return jnp.dot(a, b, precision=lax.Precision.HIGHEST, preferred_element_type=F32)


def split(v):
    high = v.astype(BF16)
    low = (v - high.astype(F32)).astype(BF16)
    return high, low


def kernel(
    n_grp, n_sub, n_low,
    load, schur, linv, basis, ginv, gm, top, fmap, spec,
    sol_out, res_out,
    stage_a, stage_s, a2, s2, perm, perm_t, b2, x2, xl2, zx2, direction, residual,
    sendb, recvb, cbuf, ubuf, qt, nmat,
    load_sem, face_send, face_recv, hi_send, hi_recv, lo_send, lo_recv, u_send, u_recv,
):
    order, columns = load.shape
    face = order // 4
    modes = basis.shape[0]
    n_high = n_sub // n_low
    g = lax.axis_index("grp")
    j = lax.axis_index("sub")
    high, low = j // n_low, j % n_low
    has = [g > 0, g < n_grp - 1, j > 0, j < n_sub - 1]
    ids = [{"grp": g - 1}, {"grp": g + 1}, {"sub": j - 1}, {"sub": j + 1}]
    weight = [jnp.where(h, 0.5, 1.0).astype(F32) for h in has]

    load_a = pltpu.make_async_copy(linv, stage_a, load_sem.at[0])
    load_s = pltpu.make_async_copy(schur, stage_s, load_sem.at[1])
    load_a.start()
    load_s.start()

    def high_peer(k):
        return lax.rem(high + k, n_high) * n_low + low

    def low_peer(k):
        return high * n_low + lax.rem(low + k, n_low)

    def grp_peer(k):
        return lax.rem(g + k, n_grp)

    barrier = pltpu.get_barrier_semaphore()
    for f in range(4):
        @pl.when(has[f])
        def _():
            pl.semaphore_signal(barrier, inc=1, device_id=ids[f], device_id_type=MESH)
    for k in range(1, n_high):
        pl.semaphore_signal(barrier, inc=1, device_id={"sub": high_peer(k)}, device_id_type=MESH)
    for k in range(1, n_low):
        pl.semaphore_signal(barrier, inc=1, device_id={"sub": low_peer(k)}, device_id_type=MESH)
    for k in range(1, n_grp):
        pl.semaphore_signal(barrier, inc=1, device_id={"grp": grp_peer(k)}, device_id_type=MESH)
    expected = (n_high - 1) + (n_low - 1) + (n_grp - 1)
    for h in has:
        expected = expected + jnp.where(h, 1, 0)
    pl.semaphore_wait(barrier, expected)

    def high_copy(r, k, owner):
        return pltpu.make_async_remote_copy(
            src_ref=cbuf.at[r, owner], dst_ref=cbuf.at[r, owner],
            send_sem=hi_send.at[r, k], recv_sem=hi_recv.at[r, k],
            device_id={"sub": high_peer(k)}, device_id_type=MESH)

    def low_copy(r, k, kh, owner):
        return pltpu.make_async_remote_copy(
            src_ref=cbuf.at[r, owner], dst_ref=cbuf.at[r, owner],
            send_sem=lo_send.at[r, k, kh], recv_sem=lo_recv.at[r, k, kh],
            device_id={"sub": low_peer(k)}, device_id_type=MESH)

    def line_owner(kh):
        return lax.rem(high + n_high - kh, n_high) * n_low + low

    def other_owner(k, kh):
        return lax.rem(high + n_high - kh, n_high) * n_low + lax.rem(low + n_low - k, n_low)

    def gather_start(r):
        for k in range(1, n_high):
            high_copy(r, k, j).start()
        for k in range(1, n_low):
            low_copy(r, k, 0, j).start()

    def gather_relay(r):
        for kh in range(1, n_high):
            high_copy(r, kh, line_owner(kh)).wait_recv()
            for k in range(1, n_low):
                low_copy(r, k, kh, line_owner(kh)).start()

    def gather_finish(r):
        for kh in range(n_high):
            for k in range(1, n_low):
                low_copy(r, k, kh, other_owner(k, kh)).wait_recv()

    def gather_drain(r):
        for k in range(1, n_high):
            high_copy(r, k, j).wait_send()
        for kh in range(n_high):
            for k in range(1, n_low):
                low_copy(r, k, kh, line_owner(kh)).wait_send()

    def u_copy(r, k, owner):
        return pltpu.make_async_remote_copy(
            src_ref=ubuf.at[r, owner], dst_ref=ubuf.at[r, owner],
            send_sem=u_send.at[r, k], recv_sem=u_recv.at[r, k],
            device_id={"grp": grp_peer(k)}, device_id_type=MESH)

    def face_copy(r, f):
        return pltpu.make_async_remote_copy(
            src_ref=sendb.at[r, f], dst_ref=recvb.at[r, f ^ 1],
            send_sem=face_send.at[r, f], recv_sem=face_recv.at[r, f ^ 1],
            device_id=ids[f], device_id_type=MESH)

    def face_wait(r, f):
        pltpu.make_async_remote_copy(
            src_ref=sendb.at[r, f], dst_ref=recvb.at[r, f],
            send_sem=face_send.at[r, f], recv_sem=face_recv.at[r, f],
            device_id=ids[f], device_id_type=MESH).wait_recv()

    def send_faces(r, depth, weighted):
        for f in range(4):
            rows = slice(f * face, (f + 1) * face)
            out = dot(perm[rows, :depth], zx2[:depth, :])
            out = out[:, :columns] + out[:, columns:]
            sendb[r, f] = out * weight[f] if weighted else out

            @pl.when(has[f])
            def _():
                face_copy(r, f).start()

    def receive_face(r, f):
        @pl.when(has[f])
        def _():
            face_wait(r, f)
            sendb_rows = sendb[r, f] + recvb[r, f]
            direct[f] = sendb_rows

        @pl.when(jnp.logical_not(has[f]))
        def _():
            direct[f] = sendb[r, f]

    direct = recvb.at[1 + 2 * ITERS]

    def to_local(total):
        def chunk(i, carry):
            rows = pl.ds(pl.multiple_of(i * face, face), face)
            second = pl.ds(pl.multiple_of(order + i * face, face), face)
            out = dot(perm_t[rows, :], x2[...])
            xl2[rows, :] = out.astype(BF16)
            xl2[second, :] = out.astype(BF16)
            if total is not None:
                total[rows, :] += out[:, :columns] + out[:, columns:]
            return carry
        lax.fori_loop(0, 4, chunk, 0)

    def apply(matrix):
        def chunk(i, carry):
            rows = pl.ds(pl.multiple_of(i * face, face), face)
            out = dot(matrix[rows, :], xl2[...])
            upper, lower = split(out[:, :columns] + out[:, columns:])
            zx2[rows, :columns] = upper
            zx2[rows, columns:] = lower
            return carry
        lax.fori_loop(0, 4, chunk, 0)

    cbuf[0, j] = jnp.zeros((modes, columns), F32)
    cbuf[0, j, :, :modes] = gm[...]
    gather_start(0)

    map_row = fmap[...]
    tile = 128

    def build_t(i, carry):
        rows = pl.ds(pl.multiple_of(i * tile, tile), tile)
        local = lax.broadcasted_iota(jnp.int32, (tile, order), 0) + i * tile
        perm_t[rows, :] = jnp.where(local == map_row, 1.0, 0.0).astype(BF16)
        return carry
    lax.fori_loop(0, order // tile, build_t, 0)
    map_column = jnp.broadcast_to(map_row.astype(F32), (tile, order)).T
    lanes = lax.broadcasted_iota(jnp.int32, (order, tile), 1).astype(F32)
    for t in range(order // tile):
        perm[:, t * tile:(t + 1) * tile] = jnp.where(
            map_column == lanes + float(t * tile), 1.0, 0.0).astype(BF16)

    def split_load(i, carry):
        rows = pl.ds(pl.multiple_of(i * face, face), face)
        upper, lower = split(load[rows, :])
        zx2[rows, :columns] = upper
        zx2[rows, columns:] = lower
        return carry
    lax.fori_loop(0, 4, split_load, 0)
    send_faces(0, order, False)

    upper, lower = split(basis[...])
    moved = dot(jnp.concatenate([upper, lower], axis=0), perm_t[...])
    b2[...] = moved.astype(BF16)
    tail = perm.shape[1] - order
    padded = jnp.concatenate([moved, jnp.zeros((tail - 2 * modes, order), F32)], axis=0)
    perm[:, order:] = padded.T.astype(BF16)
    zx2[order:, :] = jnp.zeros((tail, 2 * columns), BF16)

    def split_matrix(stage, matrix):
        def chunk(i, carry):
            rows = pl.ds(pl.multiple_of(i * tile, tile), tile)
            upper, lower = split(stage[rows, :])
            matrix[rows, :order] = upper
            matrix[rows, order:] = lower
            return carry
        lax.fori_loop(0, order // tile, chunk, 0)

    load_a.wait()
    split_matrix(stage_a, a2)
    gather_relay(0)
    load_s.wait()
    split_matrix(stage_s, s2)
    gather_finish(0)
    qt[...] = cbuf[0].reshape(n_sub * modes, columns).T[:modes, :]
    nmat[...] = exact_dot(gm[...], top[pl.ds(pl.multiple_of(g * modes, modes), modes), :])

    for f in range(4):
        receive_face(0, f)
        residual[f] = direct[f]

    sol_out[...] = jnp.zeros((order, columns), F32)
    centre = jnp.full((1, columns), 0.5 * (spec[0] + spec[1]), F32)
    half_width = jnp.full((1, columns), 0.5 * (spec[1] - spec[0]), F32)

    def precondition(r, c):
        for f in range(4):
            rows = slice(f * face, (f + 1) * face)
            upper, lower = split(residual[f] * weight[f])
            x2[rows, :columns] = upper
            x2[rows, columns:] = lower
        products = dot(b2[...], x2[...])
        products = products[:, :columns] + products[:, columns:]
        cbuf[c, j] = products[:modes, :] + products[modes:, :]
        gather_start(c)
        to_local(None)
        apply(a2)
        gather_relay(c)
        gather_finish(c)
        stacked = cbuf[c].reshape(n_sub * modes, columns)
        ubuf[c, g] = exact_dot(qt[...], stacked)
        for k in range(1, n_grp):
            u_copy(c, k, g).start()
        update = exact_dot(ginv[...], stacked)
        for k in range(1, n_grp):
            u_copy(c, k, lax.rem(g + n_grp - k, n_grp)).wait_recv()
        update = update + exact_dot(nmat[...], ubuf[c].reshape(n_grp * modes, columns))
        upper, lower = split(update)
        for base in (order, order + modes):
            zx2[base:base + modes, :columns] = upper
            zx2[base:base + modes, columns:] = lower
        send_faces(r, perm.shape[1], True)
        for f in range(4):
            receive_face(r, f)

    precondition(1, 1)
    for f in range(4):
        direction[f] = direct[f] / centre
    rho = half_width / centre
    for turn in range(ITERS):
        for f in range(4):
            rows = slice(f * face, (f + 1) * face)
            upper, lower = split(direction[f])
            x2[rows, :columns] = upper
            x2[rows, columns:] = lower
        to_local(sol_out)
        apply(s2)
        r = 2 + 2 * turn
        send_faces(r, order, False)
        for f in range(4):
            receive_face(r, f)
            residual[f] = residual[f] - direct[f]
        if turn + 1 < ITERS:
            rho_next = 1.0 / (2.0 * centre / half_width - rho)
            precondition(r + 1, 2 + turn)
            for f in range(4):
                direction[f] = rho_next * rho * direction[f] + (2.0 * rho_next / half_width) * direct[f]
            rho = rho_next

    for f in range(4):
        rows = slice(f * face, (f + 1) * face)
        upper, lower = split(residual[f])
        x2[rows, :columns] = upper
        x2[rows, columns:] = lower

    def finish(i, carry):
        rows = pl.ds(pl.multiple_of(i * face, face), face)
        out = dot(perm_t[rows, :], x2[...])
        res_out[rows, :] = out[:, :columns] + out[:, columns:]
        return carry
    lax.fori_loop(0, 4, finish, 0)

    for r in range(1 + 2 * ITERS):
        for f in range(4):
            @pl.when(has[f])
            def _():
                face_copy(r, f).wait_send()
    for c in range(1 + ITERS):
        gather_drain(c)
        if c > 0:
            for k in range(1, n_grp):
                u_copy(c, k, g).wait_send()


def solution(mesh):
    n_grp, n_sub = mesh.shape["grp"], mesh.shape["sub"]
    n_low = 1
    while n_low * n_low < n_sub:
        n_low *= 2
    n_high = n_sub // n_low

    def step(load, schur, linv, basis, ginv, gm, top, fmap, spec):
        order, columns = load.shape
        modes = basis.shape[0]
        face = order // 4
        tail = -(-2 * modes // 128) * 128
        rounds = 1 + ITERS
        faces = 1 + 2 * ITERS
        vmem = pl.BlockSpec(memory_space=pltpu.VMEM)
        hbm = pl.BlockSpec(memory_space=pl.ANY)
        smem = pl.BlockSpec(memory_space=pltpu.SMEM)
        dma = pltpu.SemaphoreType.DMA
        field = jax.ShapeDtypeStruct((order, columns), F32)
        return pl.pallas_call(
            functools.partial(kernel, n_grp, n_sub, n_low),
            out_shape=(field, field),
            in_specs=[vmem, hbm, hbm, vmem, vmem, vmem, vmem, vmem, smem],
            out_specs=(vmem, vmem),
            scratch_shapes=[
                pltpu.VMEM((order, order), F32),
                pltpu.VMEM((order, order), F32),
                pltpu.VMEM((order, 2 * order), BF16),
                pltpu.VMEM((order, 2 * order), BF16),
                pltpu.VMEM((order, order + tail), BF16),
                pltpu.VMEM((order, order), BF16),
                pltpu.VMEM((2 * modes, order), BF16),
                pltpu.VMEM((order, 2 * columns), BF16),
                pltpu.VMEM((2 * order, 2 * columns), BF16),
                pltpu.VMEM((order + tail, 2 * columns), BF16),
                pltpu.VMEM((4, face, columns), F32),
                pltpu.VMEM((4, face, columns), F32),
                pltpu.VMEM((faces, 4, face, columns), F32),
                pltpu.VMEM((faces + 1, 4, face, columns), F32),
                pltpu.VMEM((rounds, n_sub, modes, columns), F32),
                pltpu.VMEM((rounds, n_grp, modes, columns), F32),
                pltpu.VMEM((modes, n_sub * modes), F32),
                pltpu.VMEM((modes, n_grp * modes), F32),
                dma((2,)),
                dma((faces, 4)),
                dma((faces, 4)),
                dma((rounds, n_high)),
                dma((rounds, n_high)),
                dma((rounds, n_low, n_high)),
                dma((rounds, n_low, n_high)),
                dma((rounds, n_grp)),
                dma((rounds, n_grp)),
            ],
            compiler_params=pltpu.CompilerParams(
                collective_id=0, has_side_effects=True, vmem_limit_bytes=60 * 1024 * 1024
            ),
        )(load, schur, linv, basis, ginv, gm, top, fmap, spec)

    row = P(("grp", "sub"), None)
    return jax.shard_map(
        step,
        mesh=mesh,
        in_specs=(row, row, row, row, row, row, P(), row, P()),
        out_specs=(row, row),
        check_vma=False,
    )
```

profile of v0, /device:TPU:9, one launch (start us, length us, event | category | flops | bytes accessed | tf_op | source)
XLA Modules:
  0.0 107.0 jit_solution(12648027744559227890)
XLA Ops:
  0.6 102.6 %shard_map.104 = (f32[1152,128]{1,0:T(8,128)}, f32[1152,128]{1,0:T(8,128)}) custom-call(f32[1152,128]{1,0:T(8,128)} %load.1, f32[1152,1152]{1,0:T(8,128)} %schur.1, f32[1152,1152]{1,0:T(8,128)} %linv.1, f32[32,1152]{1,0:T(8,128)} %basis.1, f32[32,512]{1,0:T(8,128)} %ginv.1, f32[32,32]{1,0:T(8,128)} %gm.1, f32[64,64]{1,0:T(8,128)} %top.1, s32[1,1152]{1,0:T(1,128)} %fmap.1, ...), custom_call_target="tpu_custom_call" | custom-call | tf_op jit(solution)/shard_map/pallas_call | solution.py:345
  103.2 1.9 %copy.13 = f32[1152,128]{1,0:T(8,128)} copy(f32[1152,128]{1,0:T(8,128)} %get-tuple-element.4) | data formatting | bytes 1179648
  105.1 1.9 %copy.14 = f32[1152,128]{1,0:T(8,128)} copy(f32[1152,128]{1,0:T(8,128)} %get-tuple-element.5) | data formatting | bytes 1179648
where the time goes:
time: 107 us
  Pallas kernels  103 us (96%)
  local copies, waits for them, and re-layouts  3.83 us (4%)
    pallas_call x1, Pallas kernels, step(): pl.pallas_call(functools.partial(kernel, n_grp, n_sub, n_low), out_shape=...  103 us
    unnamed x2, local copies, waits for them, and re-layouts  3.83 us

commit v1 on v0

--- a/solution.py
+++ b/solution.py
@@ -31,9 +31,9 @@
     n_grp, n_sub, n_low,
     load, schur, linv, basis, ginv, gm, top, fmap, spec,
     sol_out, res_out,
-    stage_a, stage_s, a2, s2, perm, perm_t, b2, x2, xl2, zx2, direction, residual,
-    sendb, recvb, cbuf, ubuf, qt, nmat,
-    load_sem, face_send, face_recv, hi_send, hi_recv, lo_send, lo_recv, u_send, u_recv,
+    stage_a, stage_s, a2, s2, sp2, perm, perm_t, b2, x2, xl2, zx2, direction, residual,
+    sendb, recvb, line_modes, peer_modes, peer_rows, line, part_out, part_in, ubuf, top_in, rq, nmat,
+    load_sem, face_send, face_recv, hi_send, hi_recv, lo_send, lo_recv, k_send, k_recv, u_send, u_recv,
 ):
     order, columns = load.shape
     face = order // 4
@@ -44,6 +44,9 @@
     high, low = j // n_low, j % n_low
     has = [g > 0, g < n_grp - 1, j > 0, j < n_sub - 1]
     ids = [{"grp": g - 1}, {"grp": g + 1}, {"sub": j - 1}, {"sub": j + 1}]
+    first = jnp.where(g == 0, 1, 0)
+    third = jnp.where(j == 0, 1, 0)
+    sequence = [("grp", first), ("grp", 1 - first), ("sub", third), ("sub", 1 - third)]
     weight = [jnp.where(h, 0.5, 1.0).astype(F32) for h in has]
 
     load_a = pltpu.make_async_copy(linv, stage_a, load_sem.at[0])
@@ -69,60 +72,44 @@
         pl.semaphore_signal(barrier, inc=1, device_id={"sub": high_peer(k)}, device_id_type=MESH)
     for k in range(1, n_low):
         pl.semaphore_signal(barrier, inc=1, device_id={"sub": low_peer(k)}, device_id_type=MESH)
-    for k in range(1, n_grp):
-        pl.semaphore_signal(barrier, inc=1, device_id={"grp": grp_peer(k)}, device_id_type=MESH)
-    expected = (n_high - 1) + (n_low - 1) + (n_grp - 1)
+    for kg in range(1, n_grp):
+        for kl in range(n_low):
+            pl.semaphore_signal(
+                barrier, inc=1, device_id={"grp": grp_peer(kg), "sub": low_peer(kl)}, device_id_type=MESH)
+    expected = (n_high - 1) + (n_low - 1) + (n_grp - 1) * n_low
     for h in has:
         expected = expected + jnp.where(h, 1, 0)
     pl.semaphore_wait(barrier, expected)
 
-    def high_copy(r, k, owner):
+    def high_copy(r, k, ref, slot):
         return pltpu.make_async_remote_copy(
-            src_ref=cbuf.at[r, owner], dst_ref=cbuf.at[r, owner],
+            src_ref=ref.at[slot], dst_ref=ref.at[slot],
             send_sem=hi_send.at[r, k], recv_sem=hi_recv.at[r, k],
             device_id={"sub": high_peer(k)}, device_id_type=MESH)
 
-    def low_copy(r, k, kh, owner):
+    def setup_copy(sends, recvs, k, ref, slot):
         return pltpu.make_async_remote_copy(
-            src_ref=cbuf.at[r, owner], dst_ref=cbuf.at[r, owner],
-            send_sem=lo_send.at[r, k, kh], recv_sem=lo_recv.at[r, k, kh],
+            src_ref=ref.at[slot], dst_ref=ref.at[slot],
+            send_sem=sends, recv_sem=recvs,
             device_id={"sub": low_peer(k)}, device_id_type=MESH)
 
-    def line_owner(kh):
-        return lax.rem(high + n_high - kh, n_high) * n_low + low
-
-    def other_owner(k, kh):
-        return lax.rem(high + n_high - kh, n_high) * n_low + lax.rem(low + n_low - k, n_low)
-
-    def gather_start(r):
-        for k in range(1, n_high):
-            high_copy(r, k, j).start()
-        for k in range(1, n_low):
-            low_copy(r, k, 0, j).start()
-
-    def gather_relay(r):
-        for kh in range(1, n_high):
-            high_copy(r, kh, line_owner(kh)).wait_recv()
-            for k in range(1, n_low):
-                low_copy(r, k, kh, line_owner(kh)).start()
-
-    def gather_finish(r):
-        for kh in range(n_high):
-            for k in range(1, n_low):
-                low_copy(r, k, kh, other_owner(k, kh)).wait_recv()
-
-    def gather_drain(r):
-        for k in range(1, n_high):
-            high_copy(r, k, j).wait_send()
-        for kh in range(n_high):
-            for k in range(1, n_low):
-                low_copy(r, k, kh, line_owner(kh)).wait_send()
-
-    def u_copy(r, k, owner):
+    def part_copy(c, k):
         return pltpu.make_async_remote_copy(
-            src_ref=ubuf.at[r, owner], dst_ref=ubuf.at[r, owner],
-            send_sem=u_send.at[r, k], recv_sem=u_recv.at[r, k],
-            device_id={"grp": grp_peer(k)}, device_id_type=MESH)
+            src_ref=part_out.at[c, lax.rem(low + k, n_low)], dst_ref=part_in.at[c, k],
+            send_sem=lo_send.at[1 + c, k], recv_sem=lo_recv.at[1 + c, k],
+            device_id={"sub": low_peer(k)}, device_id_type=MESH)
+
+    def u_copy(c, kg, kl):
+        return pltpu.make_async_remote_copy(
+            src_ref=part_out.at[c, n_low], dst_ref=ubuf.at[c, kg, kl],
+            send_sem=u_send.at[c, kg, kl], recv_sem=u_recv.at[c, kg, kl],
+            device_id={"grp": grp_peer(kg), "sub": low_peer(kl)}, device_id_type=MESH)
+
+    def from_high(k):
+        return lax.rem(high + n_high - k, n_high)
+
+    def from_low(k):
+        return lax.rem(low + n_low - k, n_low)
 
     def face_copy(r, f):
         return pltpu.make_async_remote_copy(
@@ -136,16 +123,24 @@
             send_sem=face_send.at[r, f], recv_sem=face_recv.at[r, f],
             device_id=ids[f], device_id_type=MESH).wait_recv()
 
-    def send_faces(r, depth, weighted):
-        for f in range(4):
-            rows = slice(f * face, (f + 1) * face)
-            out = dot(perm[rows, :depth], zx2[:depth, :])
-            out = out[:, :columns] + out[:, columns:]
-            sendb[r, f] = out * weight[f] if weighted else out
-
-            @pl.when(has[f])
+    def each_face(r, value):
+        for axis, side in sequence:
+            f = side if axis == "grp" else side + 2
+            present = (jnp.where(side == 1, g < n_grp - 1, g > 0) if axis == "grp"
+                       else jnp.where(side == 1, j < n_sub - 1, j > 0))
+            position = (g if axis == "grp" else j) + 2 * side - 1
+            rows = pl.ds(pl.multiple_of(f * face, 16), face)
+            sendb[r, f] = value(f, rows, jnp.where(present, 0.5, 1.0).astype(F32))
+
+            @pl.when(present)
             def _():
-                face_copy(r, f).start()
+                pltpu.make_async_remote_copy(
+                    src_ref=sendb.at[r, f], dst_ref=recvb.at[r, f + 1 - 2 * side],
+                    send_sem=face_send.at[r, f], recv_sem=face_recv.at[r, f + 1 - 2 * side],
+                    device_id={axis: position}, device_id_type=MESH).start()
+
+    def halves(out):
+        return out[:, :columns] + out[:, columns:]
 
     def receive_face(r, f):
         @pl.when(has[f])
@@ -182,9 +177,15 @@
             return carry
         lax.fori_loop(0, 4, chunk, 0)
 
-    cbuf[0, j] = jnp.zeros((modes, columns), F32)
-    cbuf[0, j, :, :modes] = gm[...]
-    gather_start(0)
+    own_modes = jnp.concatenate([gm[...], jnp.zeros((modes, columns - modes), F32)], axis=1)
+    line_modes[high] = own_modes
+    peer_modes[low] = own_modes
+    peer_rows[low] = ginv[...]
+    for k in range(1, n_high):
+        high_copy(0, k, line_modes, high).start()
+    for k in range(1, n_low):
+        setup_copy(lo_send.at[0, k], lo_recv.at[0, k], k, peer_modes, low).start()
+        setup_copy(k_send.at[k], k_recv.at[k], k, peer_rows, low).start()
 
     map_row = fmap[...]
     tile = 128
@@ -208,7 +209,7 @@
         zx2[rows, columns:] = lower
         return carry
     lax.fori_loop(0, 4, split_load, 0)
-    send_faces(0, order, False)
+    each_face(0, lambda f, rows, w: halves(dot(perm[rows, :order], zx2[:order, :])))
 
     upper, lower = split(basis[...])
     moved = dot(jnp.concatenate([upper, lower], axis=0), perm_t[...])
@@ -217,6 +218,15 @@
     padded = jnp.concatenate([moved, jnp.zeros((tail - 2 * modes, order), F32)], axis=0)
     perm[:, order:] = padded.T.astype(BF16)
     zx2[order:, :] = jnp.zeros((tail, 2 * columns), BF16)
+
+    def permute_schur(start, stop):
+        def chunk(i, carry):
+            rows = pl.ds(pl.multiple_of(lax.rem(i, 4) * face, 16), face)
+            lanes = pl.ds(pl.multiple_of(i // 4 * 2 * tile, 2 * tile), 2 * tile)
+            sp2[rows, lanes] = dot(perm[rows, :order], s2[:, lanes]).astype(BF16)
+            return carry
+        lax.fori_loop(4 * start, 4 * stop, chunk, 0)
+    blocks = order // tile
 
     def split_matrix(stage, matrix):
         def chunk(i, carry):
@@ -229,12 +239,32 @@
 
     load_a.wait()
     split_matrix(stage_a, a2)
-    gather_relay(0)
     load_s.wait()
     split_matrix(stage_s, s2)
-    gather_finish(0)
-    qt[...] = cbuf[0].reshape(n_sub * modes, columns).T[:modes, :]
-    nmat[...] = exact_dot(gm[...], top[pl.ds(pl.multiple_of(g * modes, modes), modes), :])
+    for k in range(1, n_high):
+        high_copy(0, k, line_modes, from_high(k)).wait_recv()
+    for k in range(1, n_low):
+        setup_copy(lo_send.at[0, k], lo_recv.at[0, k], k, peer_modes, from_low(k)).wait_recv()
+        setup_copy(k_send.at[k], k_recv.at[k], k, peer_rows, from_low(k)).wait_recv()
+    line_t = line_modes[...].reshape(n_high * modes, columns).T[:modes, :]
+    top_rows = top[pl.ds(pl.multiple_of(g * modes, modes), modes), :]
+    top_in[...] = jnp.zeros_like(top_in)
+    own_top = pl.ds(pl.multiple_of(g * modes, modes), modes)
+    top_in[own_top, :n_high * modes] = line_t
+    lane = lax.broadcasted_iota(jnp.int32, (n_sub * modes, n_high * modes), 1)
+    target = lane + low * modes
+    for k in range(1, n_high):
+        target = target + jnp.where(lane >= k * modes, (n_low - 1) * modes, 0)
+    row = lax.broadcasted_iota(jnp.int32, (n_sub * modes, n_high * modes), 0)
+    chosen = jnp.where(row == target, 1.0, 0.0).astype(F32)
+    own_part = exact_dot(peer_rows[...].reshape(n_low * modes, n_sub * modes), chosen)
+    through = exact_dot(top_rows, top_in[:, :n_high * modes])
+    peers = peer_modes[...].reshape(n_low * modes, columns)[:, :modes]
+    rq[:n_low * modes, :] = own_part + exact_dot(peers, through)
+    rq[n_low * modes:, :] = line_t
+    nmat[...] = exact_dot(gm[...], top_rows)
+    top_in[...] = jnp.zeros_like(top_in)
+    permute_schur(0, blocks // 3)
 
     for f in range(4):
         receive_face(0, f)
@@ -252,29 +282,51 @@
             x2[rows, columns:] = lower
         products = dot(b2[...], x2[...])
         products = products[:, :columns] + products[:, columns:]
-        cbuf[c, j] = products[:modes, :] + products[modes:, :]
-        gather_start(c)
+        line[c, high] = products[:modes, :] + products[modes:, :]
+        for k in range(1, n_high):
+            high_copy(1 + c, k, line.at[c], high).start()
         to_local(None)
         apply(a2)
-        gather_relay(c)
-        gather_finish(c)
-        stacked = cbuf[c].reshape(n_sub * modes, columns)
-        ubuf[c, g] = exact_dot(qt[...], stacked)
-        for k in range(1, n_grp):
-            u_copy(c, k, g).start()
-        update = exact_dot(ginv[...], stacked)
-        for k in range(1, n_grp):
-            u_copy(c, k, lax.rem(g + n_grp - k, n_grp)).wait_recv()
-        update = update + exact_dot(nmat[...], ubuf[c].reshape(n_grp * modes, columns))
+        for k in range(1, n_high):
+            high_copy(1 + c, k, line.at[c], from_high(k)).wait_recv()
+        parts = exact_dot(rq[...], line[c].reshape(n_high * modes, columns))
+        part_out[c] = parts.reshape(n_low + 1, modes, columns)
+        for kg in range(1, n_grp):
+            for kl in range(n_low):
+                u_copy(c, kg, kl).start()
+        for k in range(1, n_low):
+            part_copy(c, k).start()
+
+        def outward(i, carry):
+            rows = pl.ds(pl.multiple_of(i * face, 16), face)
+            sendb[r, i] = halves(dot(perm[rows, :order], zx2[:order, :]))
+            return carry
+        lax.fori_loop(0, 4, outward, 0)
+        if c == 0:
+            permute_schur(blocks // 3, blocks // 2 + 1)
+        update = part_out[c, low]
+        for k in range(1, n_low):
+            part_copy(c, k).wait_recv()
+            update = update + part_in[c, k]
+        for kg in range(1, n_grp):
+            total = None
+            for kl in range(n_low):
+                u_copy(c, kg, kl).wait_recv()
+                total = ubuf[c, kg, kl] if total is None else total + ubuf[c, kg, kl]
+            source = lax.rem(g + n_grp - kg, n_grp)
+            top_in[pl.ds(pl.multiple_of(source * modes, modes), modes), :] = total
+        update = update + exact_dot(nmat[...], top_in[...])
         upper, lower = split(update)
         for base in (order, order + modes):
             zx2[base:base + modes, :columns] = upper
             zx2[base:base + modes, columns:] = lower
-        send_faces(r, perm.shape[1], True)
+        each_face(r, lambda f, rows, w: (sendb[r, f] + halves(dot(perm[rows, order:], zx2[order:, :]))) * w)
+        if c == 0:
+            permute_schur(blocks // 2 + 1, blocks)
         for f in range(4):
             receive_face(r, f)
 
-    precondition(1, 1)
+    precondition(1, 0)
     for f in range(4):
         direction[f] = direct[f] / centre
     rho = half_width / centre
@@ -285,15 +337,14 @@
             x2[rows, :columns] = upper
             x2[rows, columns:] = lower
         to_local(sol_out)
-        apply(s2)
         r = 2 + 2 * turn
-        send_faces(r, order, False)
+        each_face(r, lambda f, rows, w: halves(dot(sp2[rows, :], xl2[...])))
         for f in range(4):
             receive_face(r, f)
             residual[f] = residual[f] - direct[f]
         if turn + 1 < ITERS:
             rho_next = 1.0 / (2.0 * centre / half_width - rho)
-            precondition(r + 1, 2 + turn)
+            precondition(r + 1, 1 + turn)
             for f in range(4):
                 direction[f] = rho_next * rho * direction[f] + (2.0 * rho_next / half_width) * direct[f]
             rho = rho_next
@@ -316,11 +367,19 @@
             @pl.when(has[f])
             def _():
                 face_copy(r, f).wait_send()
-    for c in range(1 + ITERS):
-        gather_drain(c)
-        if c > 0:
-            for k in range(1, n_grp):
-                u_copy(c, k, g).wait_send()
+    for k in range(1, n_high):
+        high_copy(0, k, line_modes, high).wait_send()
+    for k in range(1, n_low):
+        setup_copy(lo_send.at[0, k], lo_recv.at[0, k], k, peer_modes, low).wait_send()
+        setup_copy(k_send.at[k], k_recv.at[k], k, peer_rows, low).wait_send()
+    for c in range(ITERS):
+        for k in range(1, n_high):
+            high_copy(1 + c, k, line.at[c], high).wait_send()
+        for k in range(1, n_low):
+            part_copy(c, k).wait_send()
+        for kg in range(1, n_grp):
+            for kl in range(n_low):
+                u_copy(c, kg, kl).wait_send()
 
 
 def solution(mesh):
@@ -352,6 +411,7 @@
                 pltpu.VMEM((order, order), F32),
                 pltpu.VMEM((order, 2 * order), BF16),
                 pltpu.VMEM((order, 2 * order), BF16),
+                pltpu.VMEM((order, 2 * order), BF16),
                 pltpu.VMEM((order, order + tail), BF16),
                 pltpu.VMEM((order, order), BF16),
                 pltpu.VMEM((2 * modes, order), BF16),
@@ -362,19 +422,27 @@
                 pltpu.VMEM((4, face, columns), F32),
                 pltpu.VMEM((faces, 4, face, columns), F32),
                 pltpu.VMEM((faces + 1, 4, face, columns), F32),
-                pltpu.VMEM((rounds, n_sub, modes, columns), F32),
-                pltpu.VMEM((rounds, n_grp, modes, columns), F32),
-                pltpu.VMEM((modes, n_sub * modes), F32),
+                pltpu.VMEM((n_high, modes, columns), F32),
+                pltpu.VMEM((n_low, modes, columns), F32),
+                pltpu.VMEM((n_low, modes, n_sub * modes), F32),
+                pltpu.VMEM((ITERS, n_high, modes, columns), F32),
+                pltpu.VMEM((ITERS, n_low + 1, modes, columns), F32),
+                pltpu.VMEM((ITERS, n_low, modes, columns), F32),
+                pltpu.VMEM((ITERS, n_grp, n_low, modes, columns), F32),
+                pltpu.VMEM((n_grp * modes, columns), F32),
+                pltpu.VMEM(((n_low + 1) * modes, n_high * modes), F32),
                 pltpu.VMEM((modes, n_grp * modes), F32),
                 dma((2,)),
                 dma((faces, 4)),
                 dma((faces, 4)),
                 dma((rounds, n_high)),
                 dma((rounds, n_high)),
-                dma((rounds, n_low, n_high)),
-                dma((rounds, n_low, n_high)),
-                dma((rounds, n_grp)),
-                dma((rounds, n_grp)),
+                dma((rounds, n_low)),
+                dma((rounds, n_low)),
+                dma((n_low,)),
+                dma((n_low,)),
+                dma((ITERS, n_grp, n_low)),
+                dma((ITERS, n_grp, n_low)),
             ],
             compiler_params=pltpu.CompilerParams(
                 collective_id=0, has_side_effects=True, vmem_limit_bytes=60 * 1024 * 1024

time: 107 us -> 97.1 us (0.907)
  Pallas kernels: 103 us -> 92.4 us
    pallas_call x1, Pallas kernels: 103 us -> 92.4 us  [step(): pl.pallas_call(functools.partial(kernel, n_grp, n_sub, n_low), out_shape=...]
where the time goes in v1:
time: 97.1 us; the launch traced here: 96.9 us
  Pallas kernels  92.4 us (95%)
  local copies, waits for them, and re-layouts  3.83 us (4%)
    pallas_call x1, Pallas kernels, step(): pl.pallas_call(functools.partial(kernel, n_grp, n_sub, n_low), out_shape=...  92.4 us
    unnamed x2, local copies, waits for them, and re-layouts  3.83 us

profile of v1, /device:TPU:9, one launch (start us, length us, event | category | flops | bytes accessed | tf_op | source)
XLA Modules:
  0.0 96.9 jit_solution(9377934804772810320)
XLA Ops:
  0.6 92.4 %shard_map.104 = (f32[1152,128]{1,0:T(8,128)}, f32[1152,128]{1,0:T(8,128)}) custom-call(f32[1152,128]{1,0:T(8,128)} %load.1, f32[1152,1152]{1,0:T(8,128)} %schur.1, f32[1152,1152]{1,0:T(8,128)} %linv.1, f32[32,1152]{1,0:T(8,128)} %basis.1, f32[32,512]{1,0:T(8,128)} %ginv.1, f32[32,32]{1,0:T(8,128)} %gm.1, f32[64,64]{1,0:T(8,128)} %top.1, s32[1,1152]{1,0:T(1,128)} %fmap.1, ...), custom_call_target="tpu_custom_call" | custom-call | tf_op jit(solution)/shard_map/pallas_call | solution.py:404
  93.1 1.9 %copy.13 = f32[1152,128]{1,0:T(8,128)} copy(f32[1152,128]{1,0:T(8,128)} %get-tuple-element.4) | data formatting | bytes 1179648
  95.0 1.9 %copy.14 = f32[1152,128]{1,0:T(8,128)} copy(f32[1152,128]{1,0:T(8,128)} %get-tuple-element.5) | data formatting | bytes 1179648

commit v2 on v1

--- a/solution.py
+++ b/solution.py
@@ -382,6 +382,11 @@
                 u_copy(c, kg, kl).wait_send()
 
 
+def hand_out(sol, res, sol_out, res_out):
+    sol_out[...] = sol[...]
+    res_out[...] = res[...]
+
+
 def solution(mesh):
     n_grp, n_sub = mesh.shape["grp"], mesh.shape["sub"]
     n_low = 1
@@ -401,7 +406,7 @@
         smem = pl.BlockSpec(memory_space=pltpu.SMEM)
         dma = pltpu.SemaphoreType.DMA
         field = jax.ShapeDtypeStruct((order, columns), F32)
-        return pl.pallas_call(
+        sol, res = pl.pallas_call(
             functools.partial(kernel, n_grp, n_sub, n_low),
             out_shape=(field, field),
             in_specs=[vmem, hbm, hbm, vmem, vmem, vmem, vmem, vmem, smem],
@@ -448,6 +453,9 @@
                 collective_id=0, has_side_effects=True, vmem_limit_bytes=60 * 1024 * 1024
             ),
         )(load, schur, linv, basis, ginv, gm, top, fmap, spec)
+        return pl.pallas_call(
+            hand_out, out_shape=(field, field), in_specs=[vmem, vmem], out_specs=(vmem, vmem)
+        )(sol, res)
 
     row = P(("grp", "sub"), None)
     return jax.shard_map(

time: 97.1 us -> 95.5 us (0.984)
  local copies, waits for them, and re-layouts: 3.83 us -> 0 us
  Pallas kernels: 92.4 us -> 94.7 us
    unnamed x2 -> x0, local copies, waits for them, and re-layouts: 3.83 us -> none
    pallas_call x0 -> x1, Pallas kernels: none -> 2.29 us  [step(): pl.pallas_call(hand_out, out_shape=(field, field), in_specs=[vmem, vmem],...]
where the time goes in v2:
time: 95.5 us; the launch traced here: 95.4 us
  Pallas kernels  94.7 us (99%)
    pallas_call x1, Pallas kernels, step(): pl.pallas_call(functools.partial(kernel, n_grp, n_sub, n_low), out_shape=...  92.4 us
    pallas_call x1, Pallas kernels, step(): pl.pallas_call(hand_out, out_shape=(field, field), in_specs=[vmem, vmem],...  2.29 us

profile of v2, /device:TPU:9, one launch (start us, length us, event | category | flops | bytes accessed | tf_op | source)
XLA Modules:
  0.0 95.4 jit_solution(9720852626397659018)
XLA Ops:
  0.6 92.4 %shard_map.104 = (f32[1152,128]{1,0:T(8,128)}, f32[1152,128]{1,0:T(8,128)}) custom-call(f32[1152,128]{1,0:T(8,128)} %load.1, f32[1152,1152]{1,0:T(8,128)} %schur.1, f32[1152,1152]{1,0:T(8,128)} %linv.1, f32[32,1152]{1,0:T(8,128)} %basis.1, f32[32,512]{1,0:T(8,128)} %ginv.1, f32[32,32]{1,0:T(8,128)} %gm.1, f32[64,64]{1,0:T(8,128)} %top.1, s32[1,1152]{1,0:T(1,128)} %fmap.1, ...), custom_call_target="tpu_custom_call" | custom-call | tf_op jit(solution)/shard_map/pallas_call | solution.py:409
  93.1 2.3 %shard_map.105 = (f32[1152,128]{1,0:T(8,128)}, f32[1152,128]{1,0:T(8,128)}) custom-call(f32[1152,128]{1,0:T(8,128)} %get-tuple-element.4.sol, f32[1152,128]{1,0:T(8,128)} %get-tuple-element.5.res), custom_call_target="tpu_custom_call" | custom-call | tf_op jit(solution)/shard_map/pallas_call | solution.py:456
